TPU v7x, 256 devices: a whole 4x4x8 slice. The times are simulated.
256 devices in a mesh: lon: 64 (over y, x_lo, z), lat: 4 (over x_hi, core).
Axes of the slice: x: 4 (x_hi: 2, x_lo: 2; x = x_hi * 2 + x_lo), y: 4, z: 8, core: 2. Of those that a mesh axis runs over, the one named last changes fastest.
Arguments:
- inputs: bfloat16 [32, 4096, 384], P('lat', 'lon'), may hold values from -16 to 16
- conv1_weight: bfloat16 [3, 3, 384, 384], replicated, may hold values from -0.109375 to 0.109375
- conv2_weight: bfloat16 [3, 3, 384, 384], replicated, may hold values from -0.109375 to 0.109375
- cotangent: bfloat16 [32, 4096, 384], P('lat', 'lon'), may hold values from -16 to 16
Outputs:
- output: bfloat16 [32, 4096, 384], P('lat', 'lon')
- input_grad: bfloat16 [32, 4096, 384], P('lat', 'lon')
- conv1_grad: float32 [3, 3, 384, 384], P(None, None, 'lon', 'lat')
- conv2_grad: float32 [3, 3, 384, 384], P(None, None, 'lon', 'lat')
All inputs are finite; a program needn't handle non-finite values.
Results may differ from a plain program's by a relative error of at most 0.0033.
Values may be sent and summed in bfloat16 or wider, within the bound.
A program may use at most 128 MiB of HBM per device.

v0:
```python
import jax
import jax.numpy as jnp
from jax import lax
from jax.sharding import PartitionSpec as P


def passed_along(shard, axis, by):
    length = lax.axis_size(axis)
    return lax.ppermute(shard, axis, [(i, (i + by) % length) for i in range(length)])


def padded(shard, sides, width):
    for axis, dim in sides:
        size, length = (lax.axis_size(axis), shard.shape[dim])
        up = [(i, (i + 1) % size) for i in range(size - 1)]
        down = [(j, i) for i, j in up]
        last = lax.slice_in_dim(shard, length - width, length, axis=dim)
        initial = lax.slice_in_dim(shard, 0, width, axis=dim)
        before = lax.ppermute(last, axis, up)
        after = lax.ppermute(initial, axis, down)
        shard = jnp.concatenate([before, shard, after], axis=dim)
    return shard


def extend(field):
    western = passed_along(field, "lon", 1)
    eastern = passed_along(field, "lon", -1)
    widened = jnp.concatenate([western, field, eastern], axis=1)
    return padded(widened, (("lat", 0),), 1)


def windows(padded_field, count_of_rows, lon_width, channels, direction):
    pieces = []
    for lat_step in (-1, 0, 1):
        for longitude_stride in (-1, 0, 1):
            row_start = 1 + direction * lat_step
            column_begin = lon_width + direction * lon_width * longitude_stride
            pieces.append(
                padded_field[
                    row_start : row_start + count_of_rows, column_begin : column_begin + lon_width
                ]
            )
    stacked = jnp.concatenate(pieces, axis=2)
    return stacked.reshape(count_of_rows * lon_width, 9 * channels)


def full_terms(stacked, grad, scale, channels):
    product = lax.dot_general(
        stacked, grad, (((0,), (0,)), ((), ())), preferred_element_type=jnp.float32
    )
    return (product * scale).reshape(9, channels, channels)


def local(inputs, conv1_weight, conv2_weight, cotangent):
    count_of_rows, lon_width, channels = inputs.shape
    cells = count_of_rows * lon_width
    lon_count = lax.axis_size("lon")
    latitude_count = lax.axis_size("lat")
    scale = (count_of_rows * latitude_count * lon_width * lon_count) ** (-0.5)
    forward_one = conv1_weight.reshape(9 * channels, channels)
    forward_two = conv2_weight.reshape(9 * channels, channels)
    turned_one = jnp.swapaxes(conv1_weight, 2, 3).reshape(9 * channels, channels)
    turned_two = jnp.swapaxes(conv2_weight, 2, 3).reshape(9 * channels, channels)
    source_field, cot_field = (inputs, cotangent)

    def stack_of(field, direction):
        return windows(extend(field), count_of_rows, lon_width, channels, direction)

    def as_field(flat):
        return flat.reshape(count_of_rows, lon_width, channels)

    stack_input = stack_of(source_field, 1)
    first = jnp.dot(stack_input, forward_one, preferred_element_type=jnp.float32)
    cdf = 0.5 * (1.0 + jax.scipy.special.erf(first / jnp.sqrt(2.0)))
    hidden = (first * cdf).astype(jnp.bfloat16)
    stack_hidden = stack_of(as_field(hidden), 1)
    second = jnp.dot(stack_hidden, forward_two, preferred_element_type=jnp.float32)
    flat_input = source_field.reshape(cells, channels)
    output = (flat_input.astype(jnp.float32) + second).astype(jnp.bfloat16)
    flat_cot = cot_field.reshape(cells, channels)
    stacked_cotangent = stack_of(cot_field, -1)
    upstream = jnp.dot(stacked_cotangent, turned_two, preferred_element_type=jnp.float32)
    density = jnp.exp(-0.5 * first * first) / jnp.sqrt(2.0 * jnp.pi)
    pre_grad = (upstream * (cdf + first * density)).astype(jnp.bfloat16)
    stack_pre = stack_of(as_field(pre_grad), -1)
    back = jnp.dot(stack_pre, turned_one, preferred_element_type=jnp.float32)
    input_grad = (flat_cot.astype(jnp.float32) + back).astype(jnp.bfloat16)
    output = output.reshape(count_of_rows, lon_width, channels)
    input_grad = input_grad.reshape(count_of_rows, lon_width, channels)
    in_part = channels // lon_count
    out_part = channels // latitude_count
    terms_one = full_terms(stack_input, pre_grad, scale, channels)
    terms_two = full_terms(stack_hidden, flat_cot, scale, channels)
    partly = (
        lax.psum_scatter(terms_one, "lon", scatter_dimension=1, tiled=True),
        lax.psum_scatter(terms_two, "lon", scatter_dimension=1, tiled=True),
    )
    grad_one, grad_two = (
        lax.psum_scatter(partly[0], "lat", scatter_dimension=2, tiled=True),
        lax.psum_scatter(partly[1], "lat", scatter_dimension=2, tiled=True),
    )
    conv1_grad = grad_one.reshape(3, 3, in_part, out_part)
    conv2_grad = grad_two.reshape(3, 3, in_part, out_part)
    return (output, input_grad, conv1_grad, conv2_grad)


def solution(mesh):
    in_specs = (P("lat", "lon", None), P(), P(), P("lat", "lon", None))
    out_specs = (
        P("lat", "lon", None),
        P("lat", "lon", None),
        P(None, None, "lon", "lat"),
        P(None, None, "lon", "lat"),
    )
    return jax.shard_map(local, mesh=mesh, in_specs=in_specs, out_specs=out_specs, check_vma=False)
```

profile of v0, /device:TPU:1, one launch (start us, length us, event | category | flops | bytes accessed | tf_op | source)
XLA Modules:
  0.0 804.9 jit_solution(5159452939540932562)
XLA Ops:
  7.2 2.5 collective-permute-start
  9.8 7.4 collective-permute-start.1
  17.2 5.7 collective-permute-start.9
  22.9 5.7 copy.10
  28.8 5.8 collective-permute-start.2
  34.6 1.9 collective-permute-start.3
  36.8 1.9 collective-permute-start.10
  38.7 5.1 collective-permute-start.11
  45.9 2.1 multiply_convert_fusion
  48.0 3.5 collective-permute-start.5
  53.5 2.1 fusion.3
  55.7 4.0 collective-permute-done.5
  59.7 6.4 collective-permute-done.4
  66.2 3.0 collective-permute-start.6
  69.2 4.4 convolution_multiply_fusion
  73.6 2.1 collective-permute-start.7
  78.4 3.1 collective-permute-done.7
  83.4 4.4 fusion
  89.4 5.8 copy.11
  96.4 2.7 collective-permute-done.13
  99.5 1.9 collective-permute-start.14
  101.4 5.1 collective-permute-start.15
  112.3 1.8 copy-done.7
  114.1 2.8 fusion.1
  116.8 572.0 %all-reduce.5.cloned.1.call-done = (f32[9,384,384]{2,1,0:T(8,128)}, f32[9,384,384]{2,1,0:T(8,128)}) async-done(((f32[9,384,384]{2,1,0:T(8,128)}, f32[9,384,384]{2,1,0:T(8,128)}), (f32[9,384,384]{2,1,0:T(8,128)}, f32[9,384,384]{2,1,0:T(8,128)})) %all-reduce.5.cloned.1.call-update) | async-done | bytes 10616848
  690.6 3.2 copy.14
  695.6 1.8 constant_dynamic-update-slice_fusion.22
  697.5 1.8 constant_dynamic-update-slice_fusion.21
  699.2 3.2 copy.18
  704.0 5.6 fusion.2
  709.6 52.7 %reduce-scatter.9.cloned.1.call-done = f32[96,54]{1,0:T(8,128)} async-done(((f32[384,54]{1,0:T(8,128)}), f32[96,54]{1,0:T(8,128)}) %reduce-scatter.9.cloned.1.call-update) | async-done | bytes 20752
  764.2 32.3 %reduce-scatter.11.cloned.1.call-done = f32[96,54]{1,0:T(8,128)} async-done(((f32[384,54]{1,0:T(8,128)}), f32[96,54]{1,0:T(8,128)}) %reduce-scatter.11.cloned.1.call-update) | async-done | bytes 20752
  (102 shorter events, 26.0 us)
Async XLA Ops:
  7.2 21.5 %copy-start.3 = (bf16[8,64,384]{2,1,0:T(8,128)(2,1)S(1)}, bf16[8,64,384]{2,1,0:T(8,128)(2,1)}, u32[]{:S(2)}) copy-start(bf16[8,64,384]{2,1,0:T(8,128)(2,1)} %param.4) | copy-start | bytes 1179652
  7.2 29.4 %copy-start.4 = (bf16[8,64,384]{2,1,0:T(8,128)(2,1)S(1)}, bf16[8,64,384]{2,1,0:T(8,128)(2,1)}, u32[]{:S(2)}) copy-start(bf16[8,64,384]{2,1,0:T(8,128)(2,1)} %param.7) | copy-start | bytes 1179652
  7.2 681.7 %all-reduce.5.cloned.1.call-start = ((), (), s32[]{:S(2)}) async-start(), calls=%async_computation.4 | async-start | bytes 21233664
  7.2 21.4 %collective-permute-start = (bf16[8,64,384]{2,1,0:T(8,128)(2,1)}, bf16[8,64,384]{2,1,0:T(8,128)(2,1)S(1)}, u32[]{:S(2)}, u32[]{:S(2)}) collective-permute-start(bf16[8,64,384]{2,1,0:T(8,128)(2,1)} %param.4), channel_id=1, source_target_pairs={{0,4},{4,8},{8,12},{12,16},{16,20},{20,24},{24,28},{28,32},{32,36}... | collective-permute-start | bytes 1179656 | tf_op jit(solution)/shard_map/ppermute | solution.py:9
  9.8 19.0 %collective-permute-start.1 = (bf16[8,64,384]{2,1,0:T(8,128)(2,1)}, bf16[8,64,384]{2,1,0:T(8,128)(2,1)S(1)}, u32[]{:S(2)}, u32[]{:S(2)}) collective-permute-start(bf16[8,64,384]{2,1,0:T(8,128)(2,1)} %param.4), channel_id=1, source_target_pairs={{0,252},{4,0},{8,4},{12,8},{16,12},{20,16},{24,20},{28,24},{32,28}... | collective-permute-start | bytes 1179656 | tf_op jit(solution)/shard_map/ppermute | solution.py:9
  17.2 19.4 %collective-permute-start.8 = (bf16[8,64,384]{2,1,0:T(8,128)(2,1)}, bf16[8,64,384]{2,1,0:T(8,128)(2,1)S(1)}, u32[]{:S(2)}, u32[]{:S(2)}) collective-permute-start(bf16[8,64,384]{2,1,0:T(8,128)(2,1)} %param.7), channel_id=1, source_target_pairs={{0,4},{4,8},{8,12},{12,16},{16,20},{20,24},{24,28},{28,32},{32,36}... | collective-permute-start | bytes 1179656 | tf_op jit(solution)/shard_map/ppermute | solution.py:9
  17.2 19.5 %collective-permute-start.9 = (bf16[8,64,384]{2,1,0:T(8,128)(2,1)}, bf16[8,64,384]{2,1,0:T(8,128)(2,1)S(1)}, u32[]{:S(2)}, u32[]{:S(2)}) collective-permute-start(bf16[8,64,384]{2,1,0:T(8,128)(2,1)} %param.7), channel_id=1, source_target_pairs={{0,252},{4,0},{8,4},{12,8},{16,12},{20,16},{24,20},{28,24},{32,28}... | collective-permute-start | bytes 1179656 | tf_op jit(solution)/shard_map/ppermute | solution.py:9
  28.8 15.0 %collective-permute-start.2 = (bf16[1,192,384]{2,1,0:T(8,128)(2,1)S(1)}, bf16[1,192,384]{2,1,0:T(8,128)(2,1)S(1)}, u32[]{:S(2)}, u32[]{:S(2)}) collective-permute-start(bf16[1,192,384]{2,1,0:T(8,128)(2,1)S(1)} %get-tuple-element.31), channel_id=1, source_target_pairs={{0,1},{1,2},{2,3},{4,5},{5,6},{6,7},{8,9},{9,10},{10,11},{12,13},{... | collective-permute-start | bytes 442376 | tf_op jit(solution)/shard_map/ppermute | solution.py:19
  34.6 9.7 %collective-permute-start.3 = (bf16[1,192,384]{2,1,0:T(8,128)(2,1)S(1)}, bf16[1,192,384]{2,1,0:T(8,128)(2,1)S(1)}, u32[]{:S(2)}, u32[]{:S(2)}) collective-permute-start(bf16[1,192,384]{2,1,0:T(8,128)(2,1)S(1)} %get-tuple-element.30), channel_id=1, source_target_pairs={{1,0},{2,1},{3,2},{5,4},{6,5},{7,6},{9,8},{10,9},{11,10},{13,12},{... | collective-permute-start | bytes 442376 | tf_op jit(solution)/shard_map/ppermute | solution.py:20
  36.8 14.7 %collective-permute-start.10 = (bf16[1,192,384]{2,1,0:T(8,128)(2,1)S(1)}, bf16[1,192,384]{2,1,0:T(8,128)(2,1)S(1)}, u32[]{:S(2)}, u32[]{:S(2)}) collective-permute-start(bf16[1,192,384]{2,1,0:T(8,128)(2,1)S(1)} %get-tuple-element.27), channel_id=1, source_target_pairs={{1,0},{2,1},{3,2},{5,4},{6,5},{7,6},{9,8},{10,9},{11,10},{13,12},{... | collective-permute-start | bytes 442376 | tf_op jit(solution)/shard_map/ppermute | solution.py:20
  38.7 13.2 %collective-permute-start.11 = (bf16[1,192,384]{2,1,0:T(8,128)(2,1)S(1)}, bf16[1,192,384]{2,1,0:T(8,128)(2,1)S(1)}, u32[]{:S(2)}, u32[]{:S(2)}) collective-permute-start(bf16[1,192,384]{2,1,0:T(8,128)(2,1)S(1)} %get-tuple-element.26), channel_id=1, source_target_pairs={{0,1},{1,2},{2,3},{4,5},{5,6},{6,7},{8,9},{9,10},{10,11},{12,13},{... | collective-permute-start | bytes 442376 | tf_op jit(solution)/shard_map/ppermute | solution.py:19
  44.2 1.8 copy-start
  48.0 11.7 %collective-permute-start.5 = (bf16[8,64,384]{2,1,0:T(8,128)(2,1)S(1)}, bf16[8,64,384]{2,1,0:T(8,128)(2,1)S(1)}, u32[]{:S(2)}, u32[]{:S(2)}) collective-permute-start(bf16[8,64,384]{2,1,0:T(8,128)(2,1)S(1)} %bitcast.65), channel_id=1, source_target_pairs={{0,252},{4,0},{8,4},{12,8},{16,12},{20,16},{24,20},{28,24},{32,28}... | collective-permute-start | bytes 1179656 | tf_op jit(solution)/shard_map/ppermute | solution.py:9
  51.5 14.6 %collective-permute-start.4 = (bf16[8,64,384]{2,1,0:T(8,128)(2,1)S(1)}, bf16[8,64,384]{2,1,0:T(8,128)(2,1)S(1)}, u32[]{:S(2)}, u32[]{:S(2)}) collective-permute-start(bf16[8,64,384]{2,1,0:T(8,128)(2,1)S(1)} %bitcast.66), channel_id=1, source_target_pairs={{0,4},{4,8},{8,12},{12,16},{16,20},{20,24},{24,28},{28,32},{32,36}... | collective-permute-start | bytes 1179656 | tf_op jit(solution)/shard_map/ppermute | solution.py:9
  51.8 1.8 copy-start.2
  66.2 9.5 %collective-permute-start.6 = (bf16[1,192,384]{2,1,0:T(8,128)(2,1)S(1)}, bf16[1,192,384]{2,1,0:T(8,128)(2,1)S(1)}, u32[]{:S(2)}, u32[]{:S(2)}) collective-permute-start(bf16[1,192,384]{2,1,0:T(8,128)(2,1)S(1)} %get-tuple-element.29), channel_id=1, source_target_pairs={{0,1},{1,2},{2,3},{4,5},{5,6},{6,7},{8,9},{9,10},{10,11},{12,13},{... | collective-permute-start | bytes 442376 | tf_op jit(solution)/shard_map/ppermute | solution.py:19
  73.6 8.0 collective-permute-start.7
  87.8 7.4 copy-start.8
  87.8 674.5 %reduce-scatter.9.cloned.1.call-start = ((), (), s32[]{:S(2)}) async-start(), calls=%async_computation.2 | async-start | bytes 245760
  87.9 11.2 %collective-permute-start.13 = (bf16[8,64,384]{2,1,0:T(8,128)(2,1)S(1)}, bf16[8,64,384]{2,1,0:T(8,128)(2,1)S(1)}, u32[]{:S(2)}, u32[]{:S(2)}) collective-permute-start(bf16[8,64,384]{2,1,0:T(8,128)(2,1)S(1)} %bitcast.77), channel_id=1, source_target_pairs={{0,252},{4,0},{8,4},{12,8},{16,12},{20,16},{24,20},{28,24},{32,28}... | collective-permute-start | bytes 1179656 | tf_op jit(solution)/shard_map/ppermute | solution.py:9
  88.0 11.5 %collective-permute-start.12 = (bf16[8,64,384]{2,1,0:T(8,128)(2,1)S(1)}, bf16[8,64,384]{2,1,0:T(8,128)(2,1)S(1)}, u32[]{:S(2)}, u32[]{:S(2)}) collective-permute-start(bf16[8,64,384]{2,1,0:T(8,128)(2,1)S(1)} %bitcast.78), channel_id=1, source_target_pairs={{0,4},{4,8},{8,12},{12,16},{16,20},{20,24},{24,28},{28,32},{32,36}... | collective-permute-start | bytes 1179656 | tf_op jit(solution)/shard_map/ppermute | solution.py:9
  99.5 10.4 %collective-permute-start.14 = (bf16[1,192,384]{2,1,0:T(8,128)(2,1)S(1)}, bf16[1,192,384]{2,1,0:T(8,128)(2,1)S(1)}, u32[]{:S(2)}, u32[]{:S(2)}) collective-permute-start(bf16[1,192,384]{2,1,0:T(8,128)(2,1)S(1)} %get-tuple-element.25), channel_id=1, source_target_pairs={{1,0},{2,1},{3,2},{5,4},{6,5},{7,6},{9,8},{10,9},{11,10},{13,12},{... | collective-permute-start | bytes 442376 | tf_op jit(solution)/shard_map/ppermute | solution.py:20
  101.4 9.8 %collective-permute-start.15 = (bf16[1,192,384]{2,1,0:T(8,128)(2,1)S(1)}, bf16[1,192,384]{2,1,0:T(8,128)(2,1)S(1)}, u32[]{:S(2)}, u32[]{:S(2)}) collective-permute-start(bf16[1,192,384]{2,1,0:T(8,128)(2,1)S(1)} %get-tuple-element.24), channel_id=1, source_target_pairs={{0,1},{1,2},{2,3},{4,5},{5,6},{6,7},{8,9},{9,10},{10,11},{12,13},{... | collective-permute-start | bytes 442376 | tf_op jit(solution)/shard_map/ppermute | solution.py:19
  109.9 1.0 copy-start.5
  110.0 1.0 copy-start.6
  110.4 3.7 copy-start.1
  112.3 1.8 copy-start.7
  695.4 101.1 %reduce-scatter.11.cloned.1.call-start = ((), (), s32[]{:S(2)}) async-start(), calls=%async_computation.3 | async-start | bytes 245760
Sparse Core Ops, SparseCore 0:
  87.9 600.8 all-reduce.4
  695.5 66.7 reduce-scatter.8
  765.2 31.2 reduce-scatter.10
where the time goes:
time: 806 us; the launch traced here: 805 us
  waiting for transfers between devices  674 us (84%)
  starting transfers between devices  47.9 us (6%)
  local copies, waits for them, and re-layouts  40.7 us (5%)
  matrix products  21.3 us (3%)
  between operations  15 us (2%)
    unnamed x6, waiting for transfers between devices  657 us
    unnamed x59, local copies, waits for them, and re-layouts  38.6 us
    ppermute x8, starting transfers between devices, passed_along(): lax.ppermute(shard, axis, [(i, (i + by) % length) for i in range(length)])  20.7 us
    ppermute x4, starting transfers between devices, padded(): before = lax.ppermute(last, axis, up)  19.1 us
  transfers between devices with their start and end apart: 19, of which 8 were waited for; matrix products, arithmetic and copies ran while one was open for 6% of the time, Pallas kernels for 0%

commit v1 on v0

v1 whole, which is shorter than its diff:
```python
import functools

import jax
import jax.numpy as jnp
import numpy as np
from jax import lax
from jax.experimental import pallas as pl
from jax.experimental.pallas import tpu as pltpu
from jax.sharding import PartitionSpec as P

MESH = pl.DeviceIdType.MESH
BF = jnp.bfloat16
F32 = jnp.float32

NY, NX, NZ = 4, 4, 8
NLON, NLAT = 64, 4
R, W, C = 8, 64, 384
TAPS, HALF = 9, 5
YC, XC, ZC = 96, 48, 6


def selection():
    pick = np.zeros((NZ * 32, HALF * XC), np.float32)
    for z in range(NZ):
        for t in range(HALF):
            for r in range(ZC):
                pick[z * 32 + t * ZC + r, t * XC + z * ZC + r] = 1.0
    return pick


def kernel(
    x_hbm, c_hbm, w1_hbm, w2_hbm, pick_ref,
    out_hbm, ig_hbm, g_hbm,
    fld, w1, w2, wt1, wt2, acc, dg, obuf, oth, oth2, ft, term,
    r1a, r1b, s1a, s1b, r2, u, zs, r3, po, go,
    ssem, rsem, osem, orem, o2s, o2r, r1s, r1r, r2s, r2r, r3s, r3r, r4s, r4r, lsem,
    *, scale,
):
    lon, lat = lax.axis_index("lon"), lax.axis_index("lat")
    y, xl, z = lon // 16, (lon // 8) % 2, lon % 8
    xh, core = lat // 2, lat % 2
    x = xh * 2 + xl
    east, west = (lon + 1) % NLON, (lon + NLON - 1) % NLON
    sib = xh * 2 + 1 - core

    def dev(o, a):
        return {"lon": o, "lat": a}

    def at_y(k):
        return dev((((y + k) % NY) * 2 + xl) * NZ + z, lat), (y + k) % NY

    def at_x(k):
        xx = (x + k) % NX
        return dev((y * 2 + xx % 2) * NZ + z, (xx // 2) * 2 + core), xx // 2, xx % 2

    def at_z(k):
        zz = (z + k) % NZ
        return dev((y * 2 + xl) * NZ + zz, lat), zz

    hbm = (x_hbm, c_hbm)
    own = [pltpu.make_async_copy(hbm[f], fld.at[f, 1, pl.ds(1, R)], lsem.at[f]) for f in range(2)]
    wload = [pltpu.make_async_copy(s, d, lsem.at[2 + i]) for i, (s, d) in enumerate(((w1_hbm, w1), (w2_hbm, w2)))]
    for cp in own + wload:
        cp.start()

    barrier = pltpu.get_barrier_semaphore()
    peers = [dev(east, lat), dev(west, lat)] + [dev(lon, (lat + k) % NLAT) for k in (1, 2, 3)]
    peers += [at_y(k)[0] for k in (1, 2, 3)] + [at_x(k)[0] for k in (1, 2, 3)] + [at_z(k)[0] for k in range(1, NZ)]
    for peer in peers:
        pl.semaphore_signal(barrier, inc=1, device_id=peer, device_id_type=MESH)
    pl.semaphore_wait(barrier, len(peers))

    def remote(src, dst, s, r, device):
        return pltpu.make_async_remote_copy(
            src_ref=src, dst_ref=dst, send_sem=s, recv_sem=r, device_id=device, device_id_type=MESH
        )

    parts = ((0, 1), (R - 1, 1), (1, R - 2))

    def ew(f, d, p):
        at, n = parts[p]
        src = hbm[f].at[pl.ds(at, n)] if f < 2 else fld.at[f, 1, pl.ds(1 + at, n)]
        k = d * 3 + p
        return remote(
            src, fld.at[f, 2 * d, pl.ds(1 + at, n)], ssem.at[f, k], rsem.at[f, k], dev(west if d else east, lat)
        )

    def ns(f, d, s):
        row = R if d else 1
        if s == 1 and f < 2:
            src = hbm[f].at[pl.ds(row - 1, 1)]
        else:
            src = fld.at[f, s, pl.ds(row, 1)]
        k = (6 if d else 9) + s
        return remote(
            src, fld.at[f, s, pl.ds(0 if d else R + 1, 1)], ssem.at[f, k], rsem.at[f, k],
            dev(lon, jnp.minimum(lat + 1, NLAT - 1) if d else jnp.maximum(lat - 1, 0)),
        )

    def north(fn):
        pl.when(lat > 0)(fn)

    def south(fn):
        pl.when(lat < NLAT - 1)(fn)

    def ns_start(f, s):
        north(lambda: ns(f, 0, s).start())
        south(lambda: ns(f, 1, s).start())

    def ns_recv(f, s):
        south(lambda: ns(f, 0, s).wait_recv())
        north(lambda: ns(f, 1, s).wait_recv())

    def ns_sent(f, s):
        north(lambda: ns(f, 0, s).wait_send())
        south(lambda: ns(f, 1, s).wait_send())

    def field_start(f):
        for p in range(3):
            for d in range(2):
                ew(f, d, p).start()
        ns_start(f, 1)

    def forward(f):
        for d in range(2):
            ew(f, d, 0).wait_recv()
            ew(f, d, 1).wait_recv()
            ns_start(f, 2 * d)

    def arrive(f, s):
        if s != 1:
            ew(f, s // 2, 2).wait_recv()
        ns_recv(f, s)

    def field_sent(f):
        for p in range(3):
            for d in range(2):
                ew(f, d, p).wait_send()
        for s in range(3):
            ns_sent(f, s)

    field_start(0)

    blank = jnp.zeros((W, C), BF)

    @pl.when(lat == 0)
    def _():
        for f in range(4):
            for s in range(3):
                fld[f, s, 0] = blank

    @pl.when(lat == NLAT - 1)
    def _():
        for f in range(4):
            for s in range(3):
                fld[f, s, R + 1] = blank

    field_start(1)

    for cp in wload:
        cp.wait()

    def turn(i, carry):
        wt2[i // 3, i % 3] = w2[i // 3, i % 3].T
        wt1[i // 3, i % 3] = w1[i // 3, i % 3].T
        return carry

    lax.fori_loop(0, TAPS, turn, 0)

    def conv_slot(f, s, weight, sign, fresh):
        b = sign * (s - 1) + 1
        taps = weight[:, b].reshape(3 * C, C)
        rows = R // 2

        def body(i, carry):
            left = jnp.concatenate(
                [
                    fld[f, s, pl.ds(1 + sign * a + rows * i, rows)].reshape(rows * W, C)
                    for a in (-1, 0, 1)
                ],
                axis=1,
            )
            part = jnp.dot(left, taps, preferred_element_type=F32).reshape(rows, W, C)
            if fresh:
                acc[pl.ds(rows * i, rows)] = part
            else:
                acc[pl.ds(rows * i, rows)] += part
            return carry

        lax.fori_loop(0, R // rows, body, 0)

    def oth_copy(f, s):
        return remote(fld.at[f, s], oth.at[s], osem.at[s], orem.at[s], dev(lon, sib))

    def oth2_copy(f):
        return remote(fld.at[f, 1, pl.ds(1, R)], oth2, o2s.at[0], o2r.at[0], dev(lon, sib))

    own[0].wait()
    forward(0)
    for i, s in enumerate((1, 0, 2)):
        arrive(0, s)

        @pl.when(core == 1)
        def _():
            oth_copy(0, s).start()

        conv_slot(0, s, w1, 1, i == 0)

    def gelu(i, carry):
        first = acc[i]
        cdf = 0.5 * (1.0 + lax.erf(first * np.float32(1 / np.sqrt(2.0))))
        fld[2, 1, 1 + i] = (first * cdf).astype(BF)
        dg[i] = cdf + first * (jnp.exp(-0.5 * first * first) * np.float32(1 / np.sqrt(2.0 * np.pi)))
        return carry

    lax.fori_loop(0, R, gelu, 0)
    field_start(2)

    @pl.when(core == 0)
    def _():
        oth2_copy(2).start()

    own[1].wait()
    forward(1)
    for i, s in enumerate((1, 0, 2)):
        arrive(1, s)

        @pl.when(core == 0)
        def _():
            oth_copy(1, s).start()

        conv_slot(1, s, wt2, -1, i == 0)

    def pre(i, carry):
        fld[3, 1, 1 + i] = (acc[i] * dg[i]).astype(BF)
        return carry

    lax.fori_loop(0, R, pre, 0)
    field_start(3)

    @pl.when(core == 1)
    def _():
        oth2_copy(3).start()

    forward(2)

    half = R * W
    ft[:, :half] = fld[3 - core, 1, pl.ds(1, R)].reshape(half, C).T
    oth2_copy(2).wait_recv()
    ft[:, half:] = oth2[...].reshape(half, C).T
    for s in range(3):
        oth_copy(0, s).wait_recv()
    sign = 1 - 2 * core

    def weight_terms(t, carry):
        slot, row = 1 + sign * (t % 3 - 1), 1 + sign * (t // 3 - 1)
        both = jnp.concatenate(
            [fld[core, slot, pl.ds(row, R)].reshape(half, C), oth[slot, pl.ds(row, R)].reshape(half, C)], axis=0
        )
        grad = jnp.dot(ft[...], both, preferred_element_type=F32)

        @pl.when(core == 0)
        def _():
            term[t] = grad.T.astype(BF).reshape(NY, 2, XC, C)

        @pl.when(core == 1)
        def _():
            term[t] = grad.astype(BF).reshape(NY, 2, XC, C)

        return carry

    lax.fori_loop(0, TAPS, weight_terms, 0)

    def first_ring(k, is_y):
        if is_y:
            device, yy = at_y(k)
            return remote(term.at[:, yy], r1a.at[k - 1], r1s.at[k - 1], r1r.at[k - 1], device)
        device, hh, ll = at_x(k)
        return remote(
            term.at[pl.ds(4 * hh, HALF), :, ll], r1b.at[k - 1], r1s.at[k - 1], r1r.at[k - 1], device
        )

    def second_ring(k, is_y):
        if is_y:
            device, yy = at_y(k)
            return remote(s1b.at[:, yy], r2.at[k - 1], r2s.at[k - 1], r2r.at[k - 1], device)
        device, hh, ll = at_x(k)
        return remote(s1a.at[pl.ds(4 * hh, HALF), ll], r2.at[k - 1], r2s.at[k - 1], r2r.at[k - 1], device)

    for c in (0, 1):

        @pl.when(core == c)
        def _():
            for k in (2, 1, 3):
                first_ring(k, c == 1).start()

    forward(3)

    def finish(f, base, weight, sgn, slot, hbm_out):
        for i, s in enumerate((1, 0, 2)):
            arrive(f, s)
            conv_slot(f, s, weight, sgn, i == 0)

        def body(i, carry):
            obuf[slot, i] = (fld[base, 1, 1 + i].astype(F32) + acc[i]).astype(BF)
            return carry

        lax.fori_loop(0, R, body, 0)
        cp = pltpu.make_async_copy(obuf.at[slot], hbm_out, lsem.at[4 + slot])
        cp.start()
        return cp

    outs = [finish(2, 0, w2, 1, 0, out_hbm), finish(3, 1, wt1, -1, 1, ig_hbm)]

    @pl.when(core == 1)
    def _():
        for k in (1, 2, 3):
            first_ring(k, True).wait_recv()

        def total(t, l):
            s = term[t, y, l].astype(F32)
            for k in range(3):
                s = s + r1a[k, t, l].astype(F32)
            return s

        def body(t, carry):
            for l in range(2):
                s1a[t, l] = total(t, l).astype(BF)
            return carry

        lax.fori_loop(0, TAPS, body, 0)
        for k in (2, 1, 3):
            second_ring(k, False).start()

        def mine(t, carry):
            u[t] = total(4 * xh + t, xl)
            return carry

        lax.fori_loop(0, HALF, mine, 0)

    @pl.when(core == 0)
    def _():
        for k in (1, 2, 3):
            first_ring(k, False).wait_recv()

        def total(t, yy):
            s = term[4 * xh + t, yy, xl].astype(F32)
            for k in range(3):
                s = s + r1b[k, t, yy].astype(F32)
            return s

        def body(t, carry):
            for yy in range(NY):
                s1b[t, yy] = total(t, yy).astype(BF)
            return carry

        lax.fori_loop(0, HALF, body, 0)
        for k in (2, 1, 3):
            second_ring(k, True).start()

        def mine(t, carry):
            u[t] = total(t, y)
            return carry

        lax.fori_loop(0, HALF, mine, 0)

    for k in (1, 2, 3):
        second_ring(k, True).wait_recv()

    summed = (u[...] + (r2[0].astype(F32) + r2[1].astype(F32) + r2[2].astype(F32))).astype(BF)
    zs[...] = (
        jnp.dot(pick_ref[...], summed.reshape(HALF * XC, C), preferred_element_type=F32).astype(BF).reshape(NZ, 32, C)
    )

    def z_copy(k):
        device, zz = at_z(k)
        return remote(zs.at[zz], r3.at[k - 1], r3s.at[k - 1], r3r.at[k - 1], device)

    for k in range(1, NZ):
        z_copy(k).start()
    q = zs[z].astype(F32)
    for k in range(1, NZ):
        z_copy(k).wait_recv()
        q = q + r3[k - 1].astype(F32)
    q = q * scale
    for l in range(NLAT):
        po[l, :, :YC] = q[:, l * YC : (l + 1) * YC]
        po[l, :, YC:] = jnp.zeros((32, 128 - YC), F32)

    def last_copy(k):
        to = (lat + k) % NLAT
        return remote(po.at[to], go.at[lat], r4s.at[k - 1], r4r.at[k - 1], dev(lon, to))

    for k in (1, 2, 3):
        last_copy(k).start()
    go[lat] = po[lat]
    for k in (1, 2, 3):
        last_copy(k).wait_recv()
    cp = pltpu.make_async_copy(go, g_hbm, lsem.at[6])
    cp.start()

    for f in range(4):
        field_sent(f)
    for s in range(3):
        oth_copy(0, s).wait_send()
    oth2_copy(2).wait_send()
    for c in (0, 1):

        @pl.when(core == c)
        def _():
            for k in (1, 2, 3):
                first_ring(k, c == 1).wait_send()
                second_ring(k, c == 0).wait_send()

    for k in range(1, NZ):
        z_copy(k).wait_send()
    for k in (1, 2, 3):
        last_copy(k).wait_send()
    for o in outs:
        o.wait()
    cp.wait()


def local(inputs, conv1_weight, conv2_weight, cotangent):
    scale = np.float32((R * NLAT * W * NLON) ** (-0.5))
    pick = jnp.asarray(selection(), BF)
    any_spec = pl.BlockSpec(memory_space=pl.ANY)
    vmem, dma = pltpu.VMEM, pltpu.SemaphoreType.DMA
    output, input_grad, g = pl.pallas_call(
        functools.partial(kernel, scale=scale),
        out_shape=[
            jax.ShapeDtypeStruct((R, W, C), BF),
            jax.ShapeDtypeStruct((R, W, C), BF),
            jax.ShapeDtypeStruct((NLAT, 32, 128), F32),
        ],
        in_specs=[any_spec] * 4 + [pl.BlockSpec(memory_space=pltpu.VMEM)],
        out_specs=[any_spec] * 3,
        scratch_shapes=[
            vmem((4, 3, R + 2, W, C), BF),
            vmem((3, 3, C, C), BF),
            vmem((3, 3, C, C), BF),
            vmem((3, 3, C, C), BF),
            vmem((3, 3, C, C), BF),
            vmem((R, W, C), F32),
            vmem((R, W, C), F32),
            vmem((2, R, W, C), BF),
            vmem((3, R + 2, W, C), BF),
            vmem((R, W, C), BF),
            vmem((C, 2 * R * W), BF),
            vmem((TAPS, NY, 2, XC, C), BF),
            vmem((3, TAPS, 2, XC, C), BF),
            vmem((3, HALF, NY, XC, C), BF),
            vmem((TAPS, 2, XC, C), BF),
            vmem((HALF, NY, XC, C), BF),
            vmem((3, HALF, XC, C), BF),
            vmem((HALF, XC, C), F32),
            vmem((NZ, 32, C), BF),
            vmem((NZ - 1, 32, C), BF),
            vmem((NLAT, 32, 128), F32),
            vmem((NLAT, 32, 128), F32),
            dma((4, 12)), dma((4, 12)),
            dma((3,)), dma((3,)),
            dma((1,)), dma((1,)),
            dma((3,)), dma((3,)),
            dma((3,)), dma((3,)),
            dma((NZ - 1,)), dma((NZ - 1,)),
            dma((3,)), dma((3,)),
            dma((7,)),
        ],
        compiler_params=pltpu.CompilerParams(
            collective_id=0, has_side_effects=True, vmem_limit_bytes=56 * 2**20
        ),
    )(inputs, cotangent, conv1_weight, conv2_weight, pick)
    rows = g[:, : HALF * ZC, :YC].reshape(NLAT, HALF, ZC, YC)
    grads = [
        jnp.concatenate([rows[c], rows[2 + c, 1:]], axis=0).reshape(3, 3, ZC, YC) for c in range(2)
    ]
    return (output, input_grad, *grads)


def solution(mesh):
    in_specs = (P("lat", "lon", None), P(), P(), P("lat", "lon", None))
    out_specs = (
        P("lat", "lon", None),
        P("lat", "lon", None),
        P(None, None, "lon", "lat"),
        P(None, None, "lon", "lat"),
    )
    return jax.shard_map(local, mesh=mesh, in_specs=in_specs, out_specs=out_specs, check_vma=False)
```

time: 806 us -> 105 us (0.13)
  waiting for transfers between devices: 674 us -> 0 us
  Pallas kernels: 0 us -> 97.1 us
  starting transfers between devices: 47.9 us -> 0 us
  local copies, waits for them, and re-layouts: 40.7 us -> 5.23 us
  matrix products: 21.3 us -> 0 us
  between operations: 15 us -> 0.66 us
    unnamed x6 -> x0, waiting for transfers between devices: 657 us -> none
    pallas_call x0 -> x1, Pallas kernels: none -> 97.1 us  [local(): pl.pallas_call(functools.partial(kernel, scale=scale), out_shape=[jax.Sha...]
    ppermute x16 -> x0, starting transfers between devices: 47.6 us -> none  [the longest x8 20.7 us: passed_along(): lax.ppermute(shard, axis, [(i, (i + by) % length) for i in range(length)])]
    unnamed x59 -> x3, local copies, waits for them, and re-layouts: 38.6 us -> 3.56 us
    dot_general x6 -> x0, matrix products: 21.3 us -> none  [the longest x2 8.79 us: full_terms(): lax.dot_general(stacked, grad, (((0,), (0,)), ((), ())), preferred_elemen...]
    ppermute x16 -> x0, waiting for transfers between devices: 16.6 us -> none  [the longest x8 13.5 us: passed_along(): lax.ppermute(shard, axis, [(i, (i + by) % length) for i in range(length)])]
  transfers between devices with their start and end apart: 19 -> 0, of which waited for: 8 -> 0; matrix products, arithmetic and copies ran while one was open for 6% -> 0% of each run, Pallas kernels for 0% -> 0%
where the time goes in v1:
time: 105 us; the launch traced here: 104 us
  Pallas kernels  97.1 us (92%)
  local copies, waits for them, and re-layouts  5.23 us (5%)
  other arithmetic  1.25 us (1%)
    pallas_call x1, Pallas kernels, local(): pl.pallas_call(functools.partial(kernel, scale=scale), out_shape=[jax.Sha...  97.1 us
    unnamed x3, local copies, waits for them, and re-layouts  3.56 us

profile of v1, /device:TPU:1, one launch (start us, length us, event | category | flops | bytes accessed | tf_op | source)
XLA Modules:
  0.0 104.2 jit_solution(10164501295208078039)
XLA Ops:
  0.6 97.1 %shard_map.84 = (bf16[8,64,384]{2,1,0:T(8,128)(2,1)}, bf16[8,64,384]{2,1,0:T(8,128)(2,1)}, f32[4,32,128]{2,1,0:T(8,128)}) custom-call(bf16[8,64,384]{2,1,0:T(8,128)(2,1)} %x_hbm.1, bf16[8,64,384]{2,1,0:T(8,128)(2,1)} %c_hbm.1, bf16[3,3,384,384]{3,2,1,0:T(8,128)(2,1)} %w1_hbm.1, bf16[3,3,384,384]{3,2,1,0:T(8,128)(2,1)} %w2_hbm.1, ...), custom_call_target="tpu_custom_call" | custom-call | tf_op jit(solution)/shard_map/pallas_call | solution.py:429
  97.7 0.9 copy.11
  98.7 0.7 fusion
  99.4 0.6 pad_maximum_fusion
  100.0 0.6 pad_maximum_fusion.1
  100.7 1.8 %copy.22 = bf16[8,64,384]{2,1,0:T(8,128)(2,1)} copy(bf16[8,64,384]{2,1,0:T(8,128)(2,1)} %get-tuple-element.18) | data formatting | bytes 786432
  102.5 1.8 %copy.23 = bf16[8,64,384]{2,1,0:T(8,128)(2,1)} copy(bf16[8,64,384]{2,1,0:T(8,128)(2,1)} %get-tuple-element.19) | data formatting | bytes 786432
  (6 shorter events, 0.0 us)

commit v2 on v1

v2 whole, which is shorter than its diff:
```python
import functools

import jax
import jax.numpy as jnp
import numpy as np
from jax import lax
from jax.experimental import pallas as pl
from jax.experimental.pallas import tpu as pltpu
from jax.sharding import PartitionSpec as P

MESH = pl.DeviceIdType.MESH
BF = jnp.bfloat16
F32 = jnp.float32

NY, NX, NZ = 4, 4, 8
NLON, NLAT, NCOL = 64, 4, 8
R, W, C = 8, 64, 384
G = W // NZ
TAPS, HALF = 9, 5
YC, XC, ZC = 96, 48, 6


def selection():
    pick = np.zeros((NZ * 32, HALF * XC), np.float32)
    for z in range(NZ):
        for t in range(HALF):
            for r in range(ZC):
                pick[z * 32 + t * ZC + r, t * XC + z * ZC + r] = 1.0
    return pick


def kernel(
    x_hbm, c_hbm, w1_hbm, w2_hbm, pick_ref,
    out_hbm, ig_hbm, g_hbm,
    fld, w1, w2, wt1, wt2, acc, dg, obuf, oth, oth2, ft, term,
    r1a, r1b, s1a, s1b, r2, u, zs, r3, po, go,
    asem, arem, hsem, hrem, osem, orem, o2s, o2r, r1s, r1r, r2s, r2r, r3s, r3r, r4s, r4r, lsem,
    *, scale,
):
    lon, lat = lax.axis_index("lon"), lax.axis_index("lat")
    y, xl, z = lon // 16, (lon // 8) % 2, lon % 8
    xh, core = lat // 2, lat % 2
    x = xh * 2 + xl
    col = lon // NZ
    east, west = (col + 1) % NCOL, (col + NCOL - 1) % NCOL
    sib = xh * 2 + 1 - core

    def dev(o, a):
        return {"lon": o, "lat": a}

    def at_y(k):
        return dev((((y + k) % NY) * 2 + xl) * NZ + z, lat), (y + k) % NY

    def at_x(k):
        xx = (x + k) % NX
        return dev((y * 2 + xx % 2) * NZ + z, (xx // 2) * 2 + core), xx // 2, xx % 2

    def at_z(k):
        zz = (z + k) % NZ
        return dev((y * 2 + xl) * NZ + zz, lat), zz

    def cols(zz):
        return pl.ds(pl.multiple_of(zz * G, G), G)

    hbm = (x_hbm, c_hbm)
    own = [
        pltpu.make_async_copy(hbm[f].at[:, cols(z)], fld.at[f, 1, pl.ds(1, R), cols(z)], lsem.at[f]) for f in range(2)
    ]
    wload = [pltpu.make_async_copy(s, d, lsem.at[2 + i]) for i, (s, d) in enumerate(((w1_hbm, w1), (w2_hbm, w2)))]
    for cp in own + wload:
        cp.start()

    barrier = pltpu.get_barrier_semaphore()
    peers = [dev(o * NZ + z, (lat + k) % NLAT) for o in (east, west) for k in (0, 1, 3)]
    peers += [dev(lon, (lat + k) % NLAT) for k in (1, 2, 3)]
    peers += [at_y(k)[0] for k in (1, 2, 3)] + [at_x(k)[0] for k in (1, 2, 3)] + [at_z(k)[0] for k in range(1, NZ)]
    for peer in peers:
        pl.semaphore_signal(barrier, inc=1, device_id=peer, device_id_type=MESH)
    pl.semaphore_wait(barrier, len(peers))

    def remote(src, dst, s, r, device):
        return pltpu.make_async_remote_copy(
            src_ref=src, dst_ref=dst, send_sem=s, recv_sem=r, device_id=device, device_id_type=MESH
        )

    order = (4, 3, 5, 2, 6, 1, 7)

    def gather(f, k):
        device, zz = at_z(k)
        return remote(
            hbm[f].at[:, cols(zz)], fld.at[f, 1, pl.ds(1, R), cols(z)], asem.at[f, k - 1], arem.at[f, k - 1], device
        )

    def give_back(f, k):
        device, zz = at_z(k)
        out = (out_hbm, ig_hbm)[f]
        return remote(
            obuf.at[f, :, cols(zz)], out.at[:, cols(z)], asem.at[2 + f, k - 1], arem.at[2 + f, k - 1], device
        )

    def halo(f, sx, sy):
        rows_from, rows_to = {0: ((1, R), 1), -1: ((1, 1), R + 1), 1: ((R, 1), 0)}[sy]
        src_cols, slot, dst_cols = {
            0: (pl.ds(0, W), 1, pl.ds(0, W)),
            1: (pl.ds(W - G, G), 0, pl.ds(0, G)),
            -1: (pl.ds(0, G), 2, pl.ds(W - G, G)),
        }[sx]
        n = rows_from[1]
        k = (sx + 1) * 3 + sy + 1
        to_lat = jnp.clip(lat + sy, 0, NLAT - 1)
        return remote(
            fld.at[f, 1, pl.ds(rows_from[0], n), src_cols], fld.at[f, slot, pl.ds(rows_to, n), dst_cols],
            hsem.at[f, k], hrem.at[f, k], dev({0: col, 1: east, -1: west}[sx] * NZ + z, to_lat),
        )

    def guarded(sy, fn, incoming):
        if sy == 0:
            fn()
        elif (sy < 0) != incoming:
            pl.when(lat > 0)(fn)
        else:
            pl.when(lat < NLAT - 1)(fn)

    sides = [(0, -1), (0, 1), (1, 0), (-1, 0), (1, -1), (1, 1), (-1, -1), (-1, 1)]

    def halo_start(f):
        for sx, sy in sides:
            guarded(sy, halo(f, sx, sy).start, False)

    def halo_sent(f):
        for sx, sy in sides:
            guarded(sy, halo(f, sx, sy).wait_send, False)

    def shift(f, rows):
        for i in rows:
            fld[f, 0, i, G:] = fld[f, 1, i, : W - G]
            fld[f, 2, i, : W - G] = fld[f, 1, i, G:]

    def arrive(f, s):
        sx = 1 - s
        for sy in (0, -1, 1):
            if sx or sy:
                guarded(sy, halo(f, sx, sy).wait_recv, True)
        if s == 1:
            shift(f, (0, R + 1))

    def gathered(f):
        for k in order:
            if f or k not in (1, 7):
                gather(f, k).wait_recv()
        own[f].wait()
        halo_start(f)
        shift(f, range(1, R + 1))

    for k in order:
        gather(0, k).start()

    blank = jnp.zeros((W, C), BF)

    @pl.when(lat == 0)
    def _():
        for f in range(4):
            for s in range(3):
                fld[f, s, 0] = blank

    @pl.when(lat == NLAT - 1)
    def _():
        for f in range(4):
            for s in range(3):
                fld[f, s, R + 1] = blank

    for cp in wload:
        cp.wait()

    def turn(i, carry):
        wt2[i // 3, i % 3] = w2[i // 3, i % 3].T
        wt1[i // 3, i % 3] = w1[i // 3, i % 3].T
        return carry

    lax.fori_loop(0, TAPS, turn, 0)

    def conv_slot(f, s, weight, sign, fresh):
        b = sign * (s - 1) + 1
        taps = weight[:, b].reshape(3 * C, C)
        left = jnp.concatenate(
            [fld[f, s, pl.ds(1 + sign * a, R)].reshape(R * W, C) for a in (-1, 0, 1)], axis=1
        )
        part = jnp.dot(left, taps, preferred_element_type=F32).reshape(R, W, C)
        if fresh:
            acc[...] = part
        else:
            acc[...] += part

    def oth_copy(f, s):
        return remote(fld.at[f, s], oth.at[s], osem.at[s], orem.at[s], dev(lon, sib))

    def oth2_copy(f):
        return remote(fld.at[f, 1, pl.ds(1, R)], oth2, o2s.at[0], o2r.at[0], dev(lon, sib))

    for k in (1, 7):
        gather(0, k).wait_recv()
    for k in order:
        gather(1, k).start()
    gathered(0)
    for i, s in enumerate((1, 0, 2)):
        arrive(0, s)

        @pl.when(core == 1)
        def _():
            oth_copy(0, s).start()

        conv_slot(0, s, w1, 1, i == 0)

    def gelu(i, carry):
        first = acc[i]
        cdf = 0.5 * (1.0 + lax.erf(first * np.float32(1 / np.sqrt(2.0))))
        fld[2, 1, 1 + i] = (first * cdf).astype(BF)
        dg[i] = cdf + first * (jnp.exp(-0.5 * first * first) * np.float32(1 / np.sqrt(2.0 * np.pi)))
        return carry

    lax.fori_loop(0, R, gelu, 0)
    halo_start(2)

    @pl.when(core == 0)
    def _():
        oth2_copy(2).start()

    shift(2, range(1, R + 1))
    gathered(1)

    def finish(f, base, weight, sgn, slot, hbm_out):
        for i, s in enumerate((1, 0, 2)):
            arrive(f, s)
            conv_slot(f, s, weight, sgn, i == 0)

        def body(i, carry):
            obuf[slot, i] = (fld[base, 1, 1 + i].astype(F32) + acc[i]).astype(BF)
            return carry

        lax.fori_loop(0, R, body, 0)
        for k in order:
            give_back(slot, k).start()
        cp = pltpu.make_async_copy(obuf.at[slot, :, cols(z)], hbm_out.at[:, cols(z)], lsem.at[4 + slot])
        cp.start()
        return cp

    outs = [finish(2, 0, w2, 1, 0, out_hbm)]

    for i, s in enumerate((1, 0, 2)):
        arrive(1, s)

        @pl.when(core == 0)
        def _():
            oth_copy(1, s).start()

        conv_slot(1, s, wt2, -1, i == 0)

    def pre(i, carry):
        fld[3, 1, 1 + i] = (acc[i] * dg[i]).astype(BF)
        return carry

    lax.fori_loop(0, R, pre, 0)
    halo_start(3)

    @pl.when(core == 1)
    def _():
        oth2_copy(3).start()

    half = R * W
    ft[:, :half] = fld[3 - core, 1, pl.ds(1, R)].reshape(half, C).T
    oth2_copy(2).wait_recv()
    ft[:, half:] = oth2[...].reshape(half, C).T
    for s in range(3):
        oth_copy(0, s).wait_recv()
    sign = 1 - 2 * core

    def weight_terms(t):
        slot, row = 1 + sign * ((t // 3 + 1) % 3 - 1), 1 + sign * (t % 3 - 1)
        both = jnp.concatenate(
            [fld[core, slot, pl.ds(row, R)].reshape(half, C), oth[slot, pl.ds(row, R)].reshape(half, C)], axis=0
        )
        grad = jnp.dot(ft[...], both, preferred_element_type=F32)

        @pl.when(core == 0)
        def _():
            term[t] = grad.T.astype(BF).reshape(NY, 2, XC, C)

        @pl.when(core == 1)
        def _():
            term[t] = grad.astype(BF).reshape(NY, 2, XC, C)

    def tap_of(p, hh):
        return jnp.minimum(2 * p + hh, TAPS - 1)

    def first_ring(p, k, is_y, n):
        sems = r1s.at[p, k - 1], r1r.at[p, k - 1]
        if is_y:
            device, yy = at_y(k)
            at = pl.ds(2 * p, n)
            return remote(term.at[at, yy], r1a.at[k - 1, at], *sems, device)
        device, hh, ll = at_x(k)
        return remote(term.at[tap_of(p, hh), :, ll], r1b.at[k - 1, p], *sems, device)

    def second_ring(p, k, is_y):
        sems = r2s.at[p, k - 1], r2r.at[p, k - 1]
        if is_y:
            device, yy = at_y(k)
            return remote(s1b.at[p, yy], r2.at[k - 1, p], *sems, device)
        device, hh, ll = at_x(k)
        return remote(s1a.at[tap_of(p, hh), ll], r2.at[k - 1, p], *sems, device)

    def piece(p, n):
        def body(i, carry):
            weight_terms(2 * p + i)
            return carry

        lax.fori_loop(0, n, body, 0)
        for c in (0, 1):

            @pl.when(core == c)
            def _():
                for k in (2, 1, 3):
                    first_ring(p, k, c == 1, n).start()

    def pieces(lo, hi):
        def body(p, carry):
            piece(p, 2)
            return carry

        lax.fori_loop(lo, hi, body, 0)

    pieces(0, 3)
    shift(3, range(1, R + 1))
    outs += [finish(3, 1, wt1, -1, 1, ig_hbm)]
    pieces(3, 4)
    piece(4, 1)

    def sum_y(p, n):
        for k in (1, 2, 3):
            first_ring(p, k, True, n).wait_recv()

        def total(t, l):
            v = term[t, y, l].astype(F32)
            for k in range(3):
                v = v + r1a[k, t, l].astype(F32)
            return v

        for i in range(n):
            for l in range(2):
                s1a[2 * p + i, l] = total(2 * p + i, l).astype(BF)
        for k in (2, 1, 3):
            second_ring(p, k, False).start()
        u[p] = total(tap_of(p, xh), xl)

    def sum_x(p, n):
        for k in (1, 2, 3):
            first_ring(p, k, False, n).wait_recv()

        def total(yy):
            v = term[tap_of(p, xh), yy, xl].astype(F32)
            for k in range(3):
                v = v + r1b[k, p, yy].astype(F32)
            return v

        for yy in range(NY):
            s1b[p, yy] = total(yy).astype(BF)
        for k in (2, 1, 3):
            second_ring(p, k, True).start()
        u[p] = total(y)

    def sums(lo, hi, n):
        for c in (0, 1):

            @pl.when(core == c)
            def _():
                def body(p, carry):
                    (sum_y if c else sum_x)(p, n)
                    return carry

                lax.fori_loop(lo, hi, body, 0)

    sums(0, 4, 2)
    sums(4, 5, 1)
    for p in range(HALF):
        for k in (1, 2, 3):
            second_ring(p, k, True).wait_recv()

    summed = (u[...] + (r2[0].astype(F32) + r2[1].astype(F32) + r2[2].astype(F32))).astype(BF)
    zs[...] = (
        jnp.dot(pick_ref[...], summed.reshape(HALF * XC, C), preferred_element_type=F32).astype(BF).reshape(NZ, 32, C)
    )

    def z_copy(k):
        device, zz = at_z(k)
        return remote(zs.at[zz], r3.at[k - 1], r3s.at[k - 1], r3r.at[k - 1], device)

    for k in range(1, NZ):
        z_copy(k).start()
    q = zs[z].astype(F32)
    for k in range(1, NZ):
        z_copy(k).wait_recv()
        q = q + r3[k - 1].astype(F32)
    q = q * scale
    for l in range(NLAT):
        po[l, :, :YC] = q[:, l * YC : (l + 1) * YC]
        po[l, :, YC:] = jnp.zeros((32, 128 - YC), F32)

    def last_copy(k):
        to = (lat + k) % NLAT
        return remote(po.at[to], go.at[lat], r4s.at[k - 1], r4r.at[k - 1], dev(lon, to))

    for k in (1, 2, 3):
        last_copy(k).start()
    go[lat] = po[lat]
    for k in (1, 2, 3):
        last_copy(k).wait_recv()
    cp = pltpu.make_async_copy(go, g_hbm, lsem.at[6])
    cp.start()

    for f in range(4):
        halo_sent(f)
    for f in range(2):
        for k in order:
            gather(f, k).wait_send()
            give_back(f, k).wait_send()
            give_back(f, k).wait_recv()
    for s in range(3):
        oth_copy(0, s).wait_send()
    oth2_copy(2).wait_send()
    for c in (0, 1):

        @pl.when(core == c)
        def _():
            for p in range(HALF):
                for k in (1, 2, 3):
                    first_ring(p, k, c == 1, 2 if p < 4 else 1).wait_send()
                    second_ring(p, k, c == 0).wait_send()

    for k in range(1, NZ):
        z_copy(k).wait_send()
    for k in (1, 2, 3):
        last_copy(k).wait_send()
    for o in outs:
        o.wait()
    cp.wait()


def place(o_ref, i_ref, g_ref, out_ref, ig_ref, g1_ref, g2_ref, sem):
    copies = [
        pltpu.make_async_copy(s, d, sem.at[i]) for i, (s, d) in enumerate(((o_ref, out_ref), (i_ref, ig_ref)))
    ]
    for cp in copies:
        cp.start()
    for t in range(TAPS):
        a, b = t % 3, (t // 3 + 1) % 3
        p, hh = t // 2, t % 2
        for c, ref in enumerate((g1_ref, g2_ref)):
            ref[a, b] = g_ref[2 * hh + c, p * ZC : (p + 1) * ZC, :YC]
    for cp in copies:
        cp.wait()


def local(inputs, conv1_weight, conv2_weight, cotangent):
    scale = np.float32((R * NLAT * W * NLON) ** (-0.5))
    pick = jnp.asarray(selection(), BF)
    any_spec = pl.BlockSpec(memory_space=pl.ANY)
    vmem, dma = pltpu.VMEM, pltpu.SemaphoreType.DMA
    output, input_grad, g = pl.pallas_call(
        functools.partial(kernel, scale=scale),
        out_shape=[
            jax.ShapeDtypeStruct((R, W, C), BF),
            jax.ShapeDtypeStruct((R, W, C), BF),
            jax.ShapeDtypeStruct((NLAT, 32, 128), F32),
        ],
        in_specs=[any_spec] * 4 + [pl.BlockSpec(memory_space=pltpu.VMEM)],
        out_specs=[any_spec] * 3,
        scratch_shapes=[
            vmem((4, 3, R + 2, W, C), BF),
            vmem((3, 3, C, C), BF),
            vmem((3, 3, C, C), BF),
            vmem((3, 3, C, C), BF),
            vmem((3, 3, C, C), BF),
            vmem((R, W, C), F32),
            vmem((R, W, C), F32),
            vmem((2, R, W, C), BF),
            vmem((3, R + 2, W, C), BF),
            vmem((R, W, C), BF),
            vmem((C, 2 * R * W), BF),
            vmem((TAPS, NY, 2, XC, C), BF),
            vmem((3, TAPS, 2, XC, C), BF),
            vmem((3, HALF, NY, XC, C), BF),
            vmem((TAPS, 2, XC, C), BF),
            vmem((HALF, NY, XC, C), BF),
            vmem((3, HALF, XC, C), BF),
            vmem((HALF, XC, C), F32),
            vmem((NZ, 32, C), BF),
            vmem((NZ - 1, 32, C), BF),
            vmem((NLAT, 32, 128), F32),
            vmem((NLAT, 32, 128), F32),
            dma((4, 7)), dma((4, 7)),
            dma((4, 9)), dma((4, 9)),
            dma((3,)), dma((3,)),
            dma((1,)), dma((1,)),
            dma((HALF, 3)), dma((HALF, 3)),
            dma((HALF, 3)), dma((HALF, 3)),
            dma((NZ - 1,)), dma((NZ - 1,)),
            dma((3,)), dma((3,)),
            dma((7,)),
        ],
        compiler_params=pltpu.CompilerParams(
            collective_id=0, has_side_effects=True, vmem_limit_bytes=56 * 2**20
        ),
    )(inputs, cotangent, conv1_weight, conv2_weight, pick)
    return pl.pallas_call(
        place,
        out_shape=[
            jax.ShapeDtypeStruct((R, W, C), BF),
            jax.ShapeDtypeStruct((R, W, C), BF),
            jax.ShapeDtypeStruct((3, 3, ZC, YC), F32),
            jax.ShapeDtypeStruct((3, 3, ZC, YC), F32),
        ],
        in_specs=[pl.BlockSpec(memory_space=pltpu.VMEM)] * 3,
        out_specs=[any_spec] * 2 + [pl.BlockSpec(memory_space=pltpu.VMEM)] * 2,
        scratch_shapes=[dma((2,))],
    )(output, input_grad, g)


def solution(mesh):
    in_specs = (P("lat", "lon", None), P(), P(), P("lat", "lon", None))
    out_specs = (
        P("lat", "lon", None),
        P("lat", "lon", None),
        P(None, None, "lon", "lat"),
        P(None, None, "lon", "lat"),
    )
    return jax.shard_map(local, mesh=mesh, in_specs=in_specs, out_specs=out_specs, check_vma=False)
```

time: 105 us -> 85.3 us (0.81)
  Pallas kernels: 97.1 us -> 84.6 us
  local copies, waits for them, and re-layouts: 5.23 us -> 0 us
  other arithmetic: 1.25 us -> 0 us
    pallas_call x1, Pallas kernels: 97.1 us -> 81.9 us  [local(): pl.pallas_call(functools.partial(kernel, scale=scale), out_shape=[jax.Sha...]
    unnamed x3 -> x0, local copies, waits for them, and re-layouts: 3.56 us -> none
    pallas_call x0 -> x1, Pallas kernels: none -> 2.64 us  [local(): pl.pallas_call(place, out_shape=[jax.ShapeDtypeStruct((R, W, C), BF), jax...]
    slice x4 -> x0, local copies, waits for them, and re-layouts: 1.65 us -> none  [the longest x1 0.88 us: local(): rows = g[:, :HALF * ZC, :YC].reshape(NLAT, HALF, ZC, YC)]
    concatenate x2 -> x0, other arithmetic: 1.25 us -> none  [local(): jnp.concatenate([rows[c], rows[2 + c, 1:]], axis=0).reshape(3, 3, ZC, YC)]
where the time goes in v2:
time: 85.3 us; the launch traced here: 85.2 us
  Pallas kernels  84.6 us (99%)
    pallas_call x1, Pallas kernels, local(): pl.pallas_call(functools.partial(kernel, scale=scale), out_shape=[jax.Sha...  81.9 us
    pallas_call x1, Pallas kernels, local(): pl.pallas_call(place, out_shape=[jax.ShapeDtypeStruct((R, W, C), BF), jax...  2.64 us

profile of v2, /device:TPU:1, one launch (start us, length us, event | category | flops | bytes accessed | tf_op | source)
XLA Modules:
  0.0 85.2 jit_solution(1611728138397410237)
XLA Ops:
  0.6 81.9 %shard_map.84 = (bf16[8,64,384]{2,1,0:T(8,128)(2,1)}, bf16[8,64,384]{2,1,0:T(8,128)(2,1)}, f32[4,32,128]{2,1,0:T(8,128)}) custom-call(bf16[8,64,384]{2,1,0:T(8,128)(2,1)} %x_hbm.1, bf16[8,64,384]{2,1,0:T(8,128)(2,1)} %c_hbm.1, bf16[3,3,384,384]{3,2,1,0:T(8,128)(2,1)} %w1_hbm.1, bf16[3,3,384,384]{3,2,1,0:T(8,128)(2,1)} %w2_hbm.1, ...), custom_call_target="tpu_custom_call" | custom-call | tf_op jit(solution)/shard_map/pallas_call | solution.py:468
  82.6 2.6 %shard_map.85 = (bf16[8,64,384]{2,1,0:T(8,128)(2,1)}, bf16[8,64,384]{2,1,0:T(8,128)(2,1)}, f32[3,3,6,96]{3,2,1,0:T(8,128)}, f32[3,3,6,96]{3,2,1,0:T(8,128)}) custom-call(bf16[8,64,384]{2,1,0:T(8,128)(2,1)} %get-tuple-element.7.o_ref, bf16[8,64,384]{2,1,0:T(8,128)(2,1)} %get-tuple-element.8.i_ref, f32[4,32,128]{2,1,0:T(8,128)} %get-tuple-element.9.g_ref), custom_call_target="tpu_custom_call" | custom-call | tf_op jit(solution)/shard_map/pallas_call | solution.py:514
